TPU v7x, 32 devices: a whole 2x2x4 slice. The times are simulated.
32 devices in a mesh: clip: 16 (over z, y, x), row: 2 (over core).
Axes of the slice: x: 2, y: 2, z: 4, core: 2. Of those that a mesh axis runs over, the one named last changes fastest.
Arguments:
- queries: bfloat16 [16, 512, 1792], P('clip', 'row'), may hold values from -36 to 36
- frames_kv: bfloat16 [16, 512, 512], P('clip', 'row'), may hold values from -20 to 20
- summary_kv: bfloat16 [16, 32, 512], P('clip', 'row'), may hold values from -6 to 6
- lengths: int32 [16], P('clip'), may hold values from 128 to 512, as said below
- caps: int32 [16], P('clip'), may hold values from 8 to 32, as said below
Outputs:
- attended: bfloat16 [16, 512, 1792], P('clip', 'row')
Inputs may be any that keep to these rules, and one draw needn't show every extreme that they name: `lengths`: some clip of every draw has 512 frame tokens. `caps`: some clip of every draw keeps 32 summary tokens.
All inputs are finite; a program needn't handle non-finite values.
Results may differ from a plain program's by a relative error of at most 0.01.
Values may be sent and summed in bfloat16 or wider, within the bound.
A program may use at most 64 MiB of HBM per device.

v0:
```python
import math
import jax
import jax.numpy as jnp
from jax import lax
from jax.sharding import PartitionSpec as P

KVH = 2
HD = 128
WINDOW = 128
masked_score = -1e30


def passed_along(block, axis, distance):
    devices = range(lax.axis_size(axis))
    route = [(i - distance, i) for i in devices if i - distance in devices]
    return lax.ppermute(block, axis, route)


def attend(state, query_heads, keys, values, valid):
    largest, total, accum = state
    scores = jnp.einsum(
        "tkgd,skd->kgts", query_heads, keys, preferred_element_type=jnp.float32
    ) * HD ** (-0.5)
    masked = jnp.where(valid, scores, masked_score)
    fresh = jnp.maximum(largest, jnp.max(masked, axis=-1))
    weights = jnp.where(valid, jnp.exp(masked - fresh[..., None]), 0.0)
    factor = jnp.exp(largest - fresh)
    total = total * factor + jnp.sum(weights, axis=-1)
    accum = accum * factor[..., None] + jnp.einsum(
        "kgts,skd->kgtd", weights.astype(jnp.bfloat16), values, preferred_element_type=jnp.float32
    )
    return (fresh, total, accum)


def split_rows(kv_rows):
    count = kv_rows.shape[0]
    keys = kv_rows[:, : KVH * HD].reshape(count, KVH, HD)
    values = kv_rows[:, KVH * HD :].reshape(count, KVH, HD)
    return (keys, values)


def fold_summary(state, piece, query_heads, clip_index):
    rows_kv, clip_caps = piece
    clip_count = rows_kv.shape[0]
    slot_count = rows_kv.shape[1]
    flat = rows_kv.reshape(clip_count * slot_count, rows_kv.shape[2])
    clip_ids = jnp.arange(clip_count)
    live = (jnp.arange(slot_count)[None, :] < clip_caps[:, None]) & (clip_ids[:, None] < clip_index)
    live = live.reshape(-1)
    count = clip_count * slot_count
    block = math.gcd(count, 512)
    blocks_kv = flat.reshape(count // block, block, flat.shape[1])
    blocks_live = live.reshape(count // block, block)

    def step_block(carry, item):
        kv_block, live_block = item
        keys, values = split_rows(kv_block)
        return (attend(carry, query_heads, keys, values, live_block), None)

    state, unused = lax.scan(step_block, state, (blocks_kv, blocks_live))
    return state


def shards(queries, frames_kv, summary_kv, lengths, caps):
    tokens_here = queries.shape[1]
    group = queries.shape[2] // (KVH * HD)
    row_index = lax.axis_index("row")
    clip_index = lax.axis_index("clip")
    own_heads = queries[0].reshape(tokens_here, KVH, group, HD)
    frames = frames_kv[0]
    rim = passed_along(frames[tokens_here - WINDOW :], "row", 1)
    local_kv = jnp.concatenate([rim, frames], axis=0)
    query_pos = row_index * tokens_here + jnp.arange(tokens_here)
    key_pos = row_index * tokens_here - WINDOW + jnp.arange(WINDOW + tokens_here)
    near = (
        (key_pos[None, :] >= 0)
        & (key_pos[None, :] <= query_pos[:, None])
        & (key_pos[None, :] > query_pos[:, None] - WINDOW)
    )
    start_state = (
        jnp.full((KVH, group, tokens_here), masked_score, jnp.float32),
        jnp.zeros((KVH, group, tokens_here), jnp.float32),
        jnp.zeros((KVH, group, tokens_here, HD), jnp.float32),
    )
    local_keys, local_values = split_rows(local_kv)
    state = attend(start_state, own_heads, local_keys, local_values, near)
    collected, every_cap = (
        lax.all_gather(summary_kv, "clip", axis=0, tiled=True),
        lax.all_gather(caps, "clip", axis=0, tiled=True),
    )
    state = fold_summary(
        state,
        (lax.all_gather(collected, "row", axis=1, tiled=True), every_cap),
        own_heads,
        clip_index,
    )
    largest, total, accum = state
    result = accum / total[..., None]
    result = jnp.transpose(result, (2, 0, 1, 3)).reshape(tokens_here, KVH * group * HD)
    result = jnp.where((query_pos < lengths[0])[:, None], result, 0.0)
    return result.astype(jnp.bfloat16)[None]


def solution(mesh):
    placed = (
        P("clip", "row", None),
        P("clip", "row", None),
        P("clip", "row", None),
        P("clip"),
        P("clip"),
    )
    return jax.shard_map(
        shards, mesh=mesh, in_specs=placed, out_specs=P("clip", "row", None), check_vma=False
    )
```

profile of v0, /device:TPU:28, one launch (start us, length us, event | category | flops | bytes accessed | tf_op | source)
XLA Modules:
  0.0 79.2 jit_solution(14224585013635414499)
XLA Ops:
  0.0 1.1 %copy.36 = bf16[1,256,512]{1,2,0:T(8,128)(2,1)S(1)} copy(bf16[1,256,512]{2,1,0:T(8,128)(2,1)} %param.6) | data formatting | bytes 524288 | tf_op args[1]
  1.1 1.7 %collective-permute-start = (bf16[128,512]{0,1:T(8,128)(2,1)S(1)}, bf16[128,512]{0,1:T(8,128)(2,1)S(1)}, u32[]{:S(2)}, u32[]{:S(2)}) collective-permute-start(bf16[128,512]{0,1:T(8,128)(2,1)S(1)} %slice_bitcast_fusion), channel_id=1, source_target_pairs={{0,1},{2,3},{4,5},{6,7},{8,9},{10,11},{12,13},{14,15},{16,17},{18,... | collective-permute-start | bytes 393224 | tf_op jit(solution)/shard_map/ppermute | solution.py:16
  2.9 36.1 %all_gather.10 = bf16[16,16,512]{2,1,0:T(8,128)(2,1)S(1)} all-gather(bf16[1,16,512]{2,1,0:T(8,128)(2,1)} %param.7), channel_id=1, replica_groups=mesh['clip'=16,'row'=2] {'clip'}, dimensions={0}, use_global_device_ids=true | all-gather | bytes 278528 | tf_op jit(solution)/shard_map/all_gather | solution.py:88
  39.0 2.2 %all_gather.11 = bf16[16,32,512]{2,1,0:T(8,128)(2,1)S(1)} all-gather(bf16[16,16,512]{2,1,0:T(8,128)(2,1)S(1)} %all_gather.10), channel_id=1, replica_groups=mesh['clip'=16,'row'=2] {'row'}, dimensions={1}, use_global_device_ids=true | all-gather | bytes 786432 | tf_op jit(solution)/shard_map/all_gather | solution.py:93
  41.8 1.2 %dynamic-slice = u32[1]{0:T(128)} dynamic-slice(u32[32]{0:T(128)} %constant.52, u32[]{:T(128)S(6)} %add.72), dynamic_slice_sizes={1} | dynamic-slice | bytes 12
  43.1 0.8 dynamic-update-slice
  43.8 16.8 %all-reduce = s32[16]{0:T(128)S(1)} all-reduce(s32[16]{0:T(128)S(1)} %dynamic-update-slice), channel_id=1, replica_groups=mesh['clip'=16,'row'=2] {'clip'}, use_global_device_ids=true, to_apply=%add | all-reduce | flops 16 | bytes 128
  60.7 0.1 fusion.23
  60.8 0.1 and.30
  60.8 0.1 copy.42
  61.0 1.5 %copy.38 = bf16[1,256,1792]{1,2,0:T(8,128)(2,1)S(1)} copy(bf16[1,256,1792]{2,1,0:T(8,128)(2,1)} %param.5) | data formatting | bytes 1835008 | tf_op args[0]
  62.5 4.3 %bitcast_reduce_fusion = (f32[2,7,256]{2,1,0:T(8,128)S(1)}, f32[2,512,256,7]{2,1,3,0:T(8,128)}) fusion(pred[512]{0:T(512)(128)(4,1)S(1)} %and.30, bf16[512,2,128,1]{0,2,3,1:T(8,128)(2,1)S(1)} %bitcast.95, bf16[256,2,7,128]{0,3,2,1:T(8,128)(2,1)S(1)} %bitcast.91), kind=kOutput, calls=%fused_computation.1 | convolution fusion | flops 475263488 | bytes 8534528 | tf_op jit(solution)/shard_map/while/body/eval_jaxpr/tkgd,skd->kgts/dot_general | solution.py:21
  66.7 0.2 compare_and_fusion
  66.9 0.1 copy.45
  67.0 0.0 copy-start
  67.9 0.0 collective-permute-done
  67.9 0.1 pad_maximum_fusion
  67.9 1.1 %fusion.4 = (f32[2,7,256]{2,1,0:T(8,128)S(1)}, f32[2,384,256,7]{2,1,3,0:T(8,128)S(1)}) fusion(pred[256,384]{0,1:T(8,128)(4,1)S(1)} %compare_and_fusion, bf16[384,2,128,1]{0,2,3,1:T(8,128)(2,1)S(1)} %bitcast.97, bf16[256,2,7,128]{0,3,2,1:T(8,128)(2,1)S(1)} %bitcast.92), kind=kOutput, calls=%fused_computation.9 | convolution fusion | flops 356446720 | bytes 6731776 | tf_op jit(solution)/shard_map/tkgd,skd->kgts/dot_general | solution.py:21
  69.0 1.1 %copy-done = f32[2,512,256,7]{2,1,3,0:T(8,128)S(1)} copy-done((f32[2,512,256,7]{2,1,3,0:T(8,128)S(1)}, f32[2,512,256,7]{2,1,3,0:T(8,128)}, u32[]{:S(2)}) %copy-start) | copy-done | bytes 7340056
  70.1 2.1 %fusion.2 = f32[2,7,256]{2,1,0:T(8,128)S(1)} fusion(f32[2,512,256,7]{2,1,3,0:T(8,128)S(1)} %copy-done, f32[2,7,256]{2,1,0:T(8,128)S(1)} %get-tuple-element.34, pred[512]{0:T(512)(128)(4,1)S(1)} %and.30), kind=kLoop, calls=%fused_computation.7 | loop fusion | flops 9171456 | bytes 7369216 | tf_op jit(solution)/shard_map/while/body/eval_jaxpr/reduce_sum | solution.py:28
  72.2 2.0 %fusion.7 = f32[2,7,256,128]{2,3,1,0:T(8,128)S(1)} fusion(bf16[512,2,128,1]{0,2,3,1:T(8,128)(2,1)S(1)} %bitcast.98, f32[2,512,256,7]{2,1,3,0:T(8,128)S(1)} %copy-done, f32[2,7,256]{2,1,0:T(8,128)S(1)} %get-tuple-element.34, pred[512]{0:T(512)(128)(4,1)S(1)} %and.30), kind=kOutput, calls=%fused_computation.12 | convolution fusion | flops 478937088 | bytes 9452032 | tf_op jit(solution)/shard_map/while/body/eval_jaxpr/kgts,skd->kgtd/dot_general | solution.py:29
  74.2 1.3 %fusion.5 = f32[2,7,256]{2,1,0:T(8,128)S(1)} fusion(f32[2,384,256,7]{2,1,3,0:T(8,128)S(1)} %get-tuple-element.36, f32[2,7,256]{2,1,0:T(8,128)S(1)} %get-tuple-element.33, pred[256,384]{0,1:T(8,128)(4,1)S(1)} %compare_and_fusion), kind=kLoop, calls=%fused_computation.10 | loop fusion | flops 6877696 | bytes 5632000 | tf_op jit(solution)/shard_map/reduce_sum | solution.py:28
  75.6 1.9 %fusion.14 = bf16[256,2,7,128]{0,3,2,1:T(8,128)(2,1)S(1)} fusion(f32[2,7,256,128]{2,3,1,0:T(8,128)S(1)} %fusion.7, bf16[384,2,128,1]{0,2,3,1:T(8,128)(2,1)S(1)} %bitcast.99, f32[2,384,256,7]{2,1,3,0:T(8,128)S(1)} %get-tuple-element.36, f32[2,7,256]{2,1,0:T(8,128)S(1)} %get-tuple-element.33, pred[256,384]{0,1:T(8,128)(4,1)S(1)} %compare_and_fusion, ...), kind=kOutput, calls=%fused_computation.18 | convolution fusion | flops 361496576 | bytes 8609792 | tf_op jit(solution)/shard_map/kgts,skd->kgtd/dot_general | solution.py:29
  77.5 0.6 copy.47
  78.1 1.1 %select_convert_fusion = bf16[1,256,1792]{2,1,0:T(8,128)(2,1)} fusion(bf16[1,256,1792]{2,1,0:T(8,128)(2,1)S(1)} %copy.47, pred[256]{0:T(512)(128)(4,1)S(1)} %fusion.25), kind=kLoop, calls=%fused_computation.21 | loop fusion | flops 458752 | bytes 1835264 | tf_op jit(solution)/shard_map/convert_element_type | solution.py:101
  (10 shorter events, 0.1 us)
Async XLA Ops:
  1.1 66.8 %collective-permute-start = (bf16[128,512]{0,1:T(8,128)(2,1)S(1)}, bf16[128,512]{0,1:T(8,128)(2,1)S(1)}, u32[]{:S(2)}, u32[]{:S(2)}) collective-permute-start(bf16[128,512]{0,1:T(8,128)(2,1)S(1)} %slice_bitcast_fusion), channel_id=1, source_target_pairs={{0,1},{2,3},{4,5},{6,7},{8,9},{10,11},{12,13},{14,15},{16,17},{18,... | collective-permute-start | bytes 393224 | tf_op jit(solution)/shard_map/ppermute | solution.py:16
  67.0 3.1 %copy-start = (f32[2,512,256,7]{2,1,3,0:T(8,128)S(1)}, f32[2,512,256,7]{2,1,3,0:T(8,128)}, u32[]{:S(2)}) copy-start(f32[2,512,256,7]{2,1,3,0:T(8,128)} %get-tuple-element.38) | copy-start | bytes 22020100
where the time goes:
time: 79.5 us; the launch traced here: 79.2 us
  blocking collectives  55.1 us (69%)
  matrix products  9.2 us (12%)
  local copies, waits for them, and re-layouts  6.69 us (8%)
  other arithmetic  4.89 us (6%)
  starting transfers between devices  1.75 us (2%)
  between operations  1.64 us (2%)
    all_gather x1, blocking collectives, shards(): lax.all_gather(summary_kv, 'clip', axis=0, tiled=True)  36.1 us
    unnamed x1, blocking collectives  16.8 us
    unnamed x7, local copies, waits for them, and re-layouts  5.66 us
    dot_general x2, matrix products, attend(): jnp.einsum('tkgd,skd->kgts', query_heads, keys, preferred_element_type=jn...  5.32 us
    dot_general x2, matrix products, attend(): jnp.einsum('kgts,skd->kgtd', weights.astype(jnp.bfloat16), values, prefer...  3.88 us
    reduce_sum x2, other arithmetic, attend(): total = total * factor + jnp.sum(weights, axis=-1)  3.38 us
    all_gather x1, blocking collectives, shards(): lax.all_gather(collected, 'row', axis=1, tiled=True)  2.17 us
    ppermute x1, starting transfers between devices, passed_along(): return lax.ppermute(block, axis, route)  1.75 us
  transfers between devices with their start and end apart: 1, of which 0 were waited for; matrix products, arithmetic and copies ran while one was open for 11% of the time, Pallas kernels for 0%

commit v1 on v0

--- a/solution.py
+++ b/solution.py
@@ -85,7 +85,9 @@
     local_keys, local_values = split_rows(local_kv)
     state = attend(start_state, own_heads, local_keys, local_values, near)
     collected, every_cap = (
-        lax.all_gather(summary_kv, "clip", axis=0, tiled=True),
+        jnp.concatenate(
+            lax.all_to_all(jnp.stack([summary_kv] * lax.axis_size("clip")), "clip", 0, 0), axis=0
+        ),
         lax.all_gather(caps, "clip", axis=0, tiled=True),
     )
     state = fold_summary(

time: 79.5 us -> 49.3 us (0.62)
  the two profiles are of different devices: /device:TPU:28 before, /device:TPU:0 now
where the time goes in v1:
time: 49.3 us; the launch traced here: 48.8 us
  blocking collectives  16.8 us (34%)
  starting transfers between devices  9.81 us (20%)
  matrix products  8.62 us (17%)
  local copies, waits for them, and re-layouts  7.15 us (15%)
  other arithmetic  4.91 us (10%)
  between operations  1.52 us (3%)
    unnamed x1, blocking collectives  14.7 us
    all_to_all x1, starting transfers between devices, shards(): lax.all_to_all(jnp.stack([summary_kv] * lax.axis_size('clip')), 'clip', 0...  8.34 us
    dot_general x2, matrix products, attend(): jnp.einsum('tkgd,skd->kgts', query_heads, keys, preferred_element_type=jn...  4.74 us
    unnamed x9, local copies, waits for them, and re-layouts  4.67 us
    dot_general x2, matrix products, attend(): jnp.einsum('kgts,skd->kgtd', weights.astype(jnp.bfloat16), values, prefer...  3.88 us
    reduce_sum x2, other arithmetic, attend(): total = total * factor + jnp.sum(weights, axis=-1)  3.4 us
    all_gather x1, blocking collectives, shards(): lax.all_gather(collected, 'row', axis=1, tiled=True)  2.17 us
    ppermute x1, starting transfers between devices, passed_along(): return lax.ppermute(block, axis, route)  1.47 us
  transfers between devices with their start and end apart: 2, of which 0 were waited for; matrix products, arithmetic and copies ran while one was open for 17% of the time, Pallas kernels for 0%

profile of v1, /device:TPU:0, one launch (start us, length us, event | category | flops | bytes accessed | tf_op | source)
XLA Modules:
  0.0 48.8 jit_solution(14289640266135084864)
XLA Ops:
  0.0 1.4 %stack.2 = bf16[16,1,16,512]{3,2,1,0:T(8,128)(2,1)} broadcast(bf16[16,512]{1,0:T(8,128)(2,1)} %bitcast.105), dimensions={2,3} | broadcast | bytes 278528 | tf_op jit(solution)/shard_map/stack | solution.py:89
  1.4 8.3 %all-to-all-start = ((bf16[16,1,16,512]{3,2,1,0:T(8,128)(2,1)}), bf16[16,1,16,512]{3,2,1,0:T(8,128)(2,1)S(1)}, u32[]{:S(2)}, u32[]{:S(2)}) async-start(bf16[16,1,16,512]{3,2,1,0:T(8,128)(2,1)} %stack.2), calls=%async_computation | async-start | bytes 524288 | tf_op jit(solution)/shard_map/all_to_all | solution.py:89
  9.8 1.1 %copy.25 = bf16[1,256,512]{1,2,0:T(8,128)(2,1)S(1)} copy(bf16[1,256,512]{2,1,0:T(8,128)(2,1)} %param.6) | data formatting | bytes 524288 | tf_op args[1]
  10.9 1.5 %collective-permute-start = (bf16[128,512]{0,1:T(8,128)(2,1)S(1)}, bf16[128,512]{0,1:T(8,128)(2,1)S(1)}, u32[]{:S(2)}, u32[]{:S(2)}) collective-permute-start(bf16[128,512]{0,1:T(8,128)(2,1)S(1)} %slice_bitcast_fusion), channel_id=1, source_target_pairs={{0,1},{2,3},{4,5},{6,7},{8,9},{10,11},{12,13},{14,15},{16,17},{18,... | collective-permute-start | bytes 393224 | tf_op jit(solution)/shard_map/ppermute | solution.py:16
  13.1 1.3 %dynamic-slice = u32[1]{0:T(128)} dynamic-slice(u32[32]{0:T(128)} %constant.52, u32[]{:T(128)S(6)} %add.72), dynamic_slice_sizes={1} | dynamic-slice | bytes 12
  14.4 0.8 %dynamic-update-slice = s32[16]{0:T(128)S(1)} dynamic-update-slice(s32[16]{0:T(128)S(1)} %broadcast.120, s32[1]{0:T(128)S(6)} %copy.52, u32[]{:T(128)} %bitcast.12) | dynamic-update-slice | bytes 12
  15.2 14.7 %all-reduce = s32[16]{0:T(128)S(1)} all-reduce(s32[16]{0:T(128)S(1)} %dynamic-update-slice), channel_id=1, replica_groups=mesh['clip'=16,'row'=2] {'clip'}, use_global_device_ids=true, to_apply=%add | all-reduce | flops 16 | bytes 128
  29.9 0.2 compare_and_fusion
  30.1 0.1 fusion.23
  30.1 0.1 and.30
  30.2 1.5 %copy.27 = bf16[1,256,1792]{1,2,0:T(8,128)(2,1)S(1)} copy(bf16[1,256,1792]{2,1,0:T(8,128)(2,1)} %param.5) | data formatting | bytes 1835008 | tf_op args[0]
  32.3 0.0 collective-permute-done
  32.4 0.1 pad_maximum_fusion
  32.4 3.4 %fusion.4 = (f32[2,7,256]{2,1,0:T(8,128)S(1)}, f32[2,384,256,7]{2,1,3,0:T(8,128)}) fusion(pred[256,384]{0,1:T(8,128)(4,1)S(1)} %compare_and_fusion, bf16[384,2,128,1]{0,2,3,1:T(8,128)(2,1)S(1)} %bitcast.102, bf16[256,2,7,128]{0,3,2,1:T(8,128)(2,1)S(1)} %bitcast.95), kind=kOutput, calls=%fused_computation.9 | convolution fusion | flops 356446720 | bytes 6731776 | tf_op jit(solution)/shard_map/tkgd,skd->kgts/dot_general | solution.py:21
  35.8 0.0 all-to-all-done
  35.8 2.2 %all-gather = bf16[16,1,32,512]{3,2,0,1:T(8,128)(2,1)S(1)} all-gather(bf16[16,1,16,512]{3,2,0,1:T(8,128)(2,1)S(1)} %bitcast.99), channel_id=2, replica_groups=mesh['clip'=16,'row'=2] {'row'}, dimensions={2}, use_global_device_ids=true | all-gather | bytes 786432 | tf_op jit(solution)/shard_map/all_gather | solution.py:95
  38.0 0.1 copy.35
  38.2 0.1 copy.32
  38.3 1.3 %bitcast_reduce_fusion = (f32[2,7,256]{2,1,0:T(8,128)S(1)}, f32[2,512,256,7]{2,1,3,0:T(8,128)S(1)}) fusion(pred[512]{0:T(512)(128)(4,1)S(1)} %and.30, bf16[512,2,128,1]{0,2,3,1:T(8,128)(2,1)S(1)} %bitcast.100, bf16[256,2,7,128]{0,3,2,1:T(8,128)(2,1)S(1)} %bitcast.96), kind=kOutput, calls=%fused_computation.1 | convolution fusion | flops 475263488 | bytes 8534528 | tf_op jit(solution)/shard_map/while/body/eval_jaxpr/tkgd,skd->kgts/dot_general | solution.py:21
  39.7 0.0 slice-start
  39.7 2.1 %fusion.2 = f32[2,7,256]{2,1,0:T(8,128)S(1)} fusion(f32[2,512,256,7]{2,1,3,0:T(8,128)S(1)} %get-tuple-element.38, f32[2,7,256]{2,1,0:T(8,128)S(1)} %get-tuple-element.34, pred[512]{0:T(512)(128)(4,1)S(1)} %and.30), kind=kLoop, calls=%fused_computation.7 | loop fusion | flops 9171456 | bytes 7369216 | tf_op jit(solution)/shard_map/while/body/eval_jaxpr/reduce_sum | solution.py:28
  41.8 0.0 slice-start.1
  41.8 2.0 %fusion.7 = f32[2,7,256,128]{2,3,1,0:T(8,128)S(1)} fusion(bf16[512,2,128,1]{0,2,3,1:T(8,128)(2,1)S(1)} %bitcast.103, f32[2,512,256,7]{2,1,3,0:T(8,128)S(1)} %get-tuple-element.38, f32[2,7,256]{2,1,0:T(8,128)S(1)} %get-tuple-element.34, pred[512]{0:T(512)(128)(4,1)S(1)} %and.30), kind=kOutput, calls=%fused_computation.12 | convolution fusion | flops 478937088 | bytes 9452032 | tf_op jit(solution)/shard_map/while/body/eval_jaxpr/kgts,skd->kgtd/dot_general | solution.py:29
  43.8 0.0 slice-done
  43.8 0.0 slice-done.1
  43.8 1.3 %fusion.5 = f32[2,7,256]{2,1,0:T(8,128)S(1)} fusion(f32[2,384,256,7]{2,1,3,0:T(8,128)S(1)} %bitcast.94, f32[2,7,256]{2,1,0:T(8,128)S(1)} %get-tuple-element.33, pred[256,384]{0,1:T(8,128)(4,1)S(1)} %compare_and_fusion), kind=kLoop, calls=%fused_computation.10 | loop fusion | flops 6877696 | bytes 5632000 | tf_op jit(solution)/shard_map/reduce_sum | solution.py:28
  45.2 1.9 %fusion.14 = bf16[256,2,7,128]{0,3,2,1:T(8,128)(2,1)S(1)} fusion(f32[2,7,256,128]{2,3,1,0:T(8,128)S(1)} %fusion.7, bf16[384,2,128,1]{0,2,3,1:T(8,128)(2,1)S(1)} %bitcast.104, f32[2,384,256,7]{2,1,3,0:T(8,128)S(1)} %bitcast.94, f32[2,7,256]{2,1,0:T(8,128)S(1)} %get-tuple-element.33, pred[256,384]{0,1:T(8,128)(4,1)S(1)} %compare_and_fusion, ...), kind=kOutput, calls=%fused_computation.18 | convolution fusion | flops 361496576 | bytes 8609792 | tf_op jit(solution)/shard_map/kgts,skd->kgtd/dot_general | solution.py:29
  47.1 0.6 %copy.37 = bf16[1,256,1792]{2,1,0:T(8,128)(2,1)S(1)} copy(bf16[1,256,1792]{1,2,0:T(8,128)(2,1)S(1)} %bitcast.101) | data formatting | bytes 1835008 | tf_op jit(solution)/shard_map/reshape | solution.py:101
  47.7 1.1 %select_convert_fusion = bf16[1,256,1792]{2,1,0:T(8,128)(2,1)} fusion(bf16[1,256,1792]{2,1,0:T(8,128)(2,1)S(1)} %copy.37, pred[256]{0:T(512)(128)(4,1)S(1)} %fusion.25), kind=kLoop, calls=%fused_computation.21 | loop fusion | flops 458752 | bytes 1835264 | tf_op jit(solution)/shard_map/convert_element_type | solution.py:103
  (11 shorter events, 0.1 us)
Async XLA Ops:
  1.4 34.4 %all-to-all-start = ((bf16[16,1,16,512]{3,2,1,0:T(8,128)(2,1)}), bf16[16,1,16,512]{3,2,1,0:T(8,128)(2,1)S(1)}, u32[]{:S(2)}, u32[]{:S(2)}) async-start(bf16[16,1,16,512]{3,2,1,0:T(8,128)(2,1)} %stack.2), calls=%async_computation | async-start | bytes 524288 | tf_op jit(solution)/shard_map/all_to_all | solution.py:89
  10.9 21.4 %collective-permute-start = (bf16[128,512]{0,1:T(8,128)(2,1)S(1)}, bf16[128,512]{0,1:T(8,128)(2,1)S(1)}, u32[]{:S(2)}, u32[]{:S(2)}) collective-permute-start(bf16[128,512]{0,1:T(8,128)(2,1)S(1)} %slice_bitcast_fusion), channel_id=1, source_target_pairs={{0,1},{2,3},{4,5},{6,7},{8,9},{10,11},{12,13},{14,15},{16,17},{18,... | collective-permute-start | bytes 393224 | tf_op jit(solution)/shard_map/ppermute | solution.py:16
  39.7 4.1 %slice-start = ((s8[5505024]{0:T(1024)(128)(4,1)}), s8[4194304]{0:T(1024)(128)(4,1)S(1)}, s32[]{:S(2)}) async-start(s8[5505024]{0:T(1024)(128)(4,1)} %bitcast.93), calls=%async_computation.1 | async-start | bytes 8388608
  41.8 2.0 %slice-start.1 = ((s8[5505024]{0:T(1024)(128)(4,1)}), s8[1310720]{0:T(1024)(128)(4,1)S(1)}, s32[]{:S(2)}) async-start(s8[5505024]{0:T(1024)(128)(4,1)} %bitcast.93), calls=%async_computation.2 | async-start | bytes 2621440
